TPU v7x, 512 devices: a whole 4x8x8 slice. The times are simulated.
512 devices in a mesh: lon: 32 (over x, y_hi, core), head: 16 (over z, y_lo).
Axes of the slice: x: 4, y: 8 (y_hi: 4, y_lo: 2; y = y_hi * 2 + y_lo), z: 8, core: 2. Of those that a mesh axis runs over, the one named last changes fastest.
Arguments:
- latents: bfloat16 [3, 48, 256, 1024], P(None, 'head', 'lon'), may hold values from -16 to 16
- out_grad: bfloat16 [3, 48, 256, 1024], P(None, 'head', 'lon'), may hold values from -6 to 6
- qkv_weight: bfloat16 [16, 1024, 192], P('head'), as said below
- out_weight: bfloat16 [16, 64, 1024], replicated, may hold values from -0.1875 to 0.1875
Outputs:
- mixed: bfloat16 [3, 48, 256, 1024], P(None, 'head', 'lon')
- latent_grad: bfloat16 [3, 48, 256, 1024], P(None, 'head', 'lon')
- qkv_grad: float32 [16, 1024, 192], P('head')
Inputs may be any that keep to these rules, and one draw needn't show every extreme that they name: `qkv_weight`: entries lie within -14 / sqrt(1024) and 14 / sqrt(1024).
All inputs are finite; a program needn't handle non-finite values.
Results may differ from a plain program's by a relative error of at most 0.024.
The roundings to bfloat16 on the way count: a program that leaves them out, or rounds other values in their place, can miss the bound.
Values may be sent and summed in bfloat16 or wider, within the bound.
No kernel may reach another device: no remote copies, remote signals or barrier semaphores. Data moves between devices by JAX's collectives and lax.ppermute only.
A program may use at most 64 MiB of HBM per device.

v0:
```python
import jax
import jax.numpy as jnp
from jax import lax
from jax.sharding import PartitionSpec as P

WIN_LAT = 6
WIN_LON = 8
MASKED = -1e30


def extended(block, sides, width):
    for axis, dim in sides:
        count = lax.axis_size(axis)
        forward = [(i, i + 1) for i in range(count - 1)]
        forward.append((count - 1, 0))
        backward = [(target, source) for source, target in forward]
        low = lax.ppermute(
            lax.slice_in_dim(block, block.shape[dim] - width, None, axis=dim), axis, forward
        )
        high = lax.ppermute(lax.slice_in_dim(block, 0, width, axis=dim), axis, backward)
        block = jnp.concatenate([low, block, high], axis=dim)
    return block


def shifted(block, axis, distance):
    devices = range(lax.axis_size(axis))
    route = [((i - distance) % len(devices), i) for i in devices]
    return lax.ppermute(block, axis, route)


def softmax_rows(query_rows, key_rows, valid, score_scale_factor):
    score_matrix = (
        jnp.einsum("fud,fwd->fuw", query_rows, key_rows, preferred_element_type=jnp.float32)
        * score_scale_factor
    )
    score_matrix = jnp.where(valid[:, None, :], score_matrix, MASKED)
    row_max = jnp.max(score_matrix, axis=-1, keepdims=True)
    powers = jnp.exp(score_matrix - row_max)
    return powers / jnp.sum(powers, axis=-1, keepdims=True)


def attend_block(pack, head_width, score_scale_factor):
    query_rows, key_value_pairs, valid = pack
    probs = softmax_rows(query_rows, key_value_pairs[..., :head_width], valid, score_scale_factor)
    probabilities_bfloat = probs.astype(jnp.bfloat16)
    attended_values = jnp.einsum(
        "ucf,ufg->ucg",
        probabilities_bfloat,
        key_value_pairs[..., head_width:],
        preferred_element_type=jnp.float32,
    )
    return attended_values.astype(jnp.bfloat16)


def attend_grad(pack, head_width, score_scale_factor):
    query_rows, key_value_pairs, valid, outer_gradient = pack
    key_portion = key_value_pairs[..., :head_width]
    value_portion = key_value_pairs[..., head_width:]
    probs = softmax_rows(query_rows, key_portion, valid, score_scale_factor)
    probabilities_bfloat = probs.astype(jnp.bfloat16)
    probability_gradient = jnp.einsum(
        "fud,fwd->fuw", outer_gradient, value_portion, preferred_element_type=jnp.float32
    )
    centre = jnp.sum(probs * probability_gradient, axis=-1, keepdims=True)
    score_gradient = (probs * (probability_gradient - centre)).astype(jnp.bfloat16)
    query_gradient = (
        jnp.einsum("ucf,ufg->ucg", score_gradient, key_portion, preferred_element_type=jnp.float32)
        * score_scale_factor
    )
    key_gradient = (
        jnp.einsum("txd,txr->tdr", score_gradient, query_rows, preferred_element_type=jnp.float32)
        * score_scale_factor
    )
    value_gradient = jnp.einsum(
        "txd,txr->tdr", probabilities_bfloat, outer_gradient, preferred_element_type=jnp.float32
    )
    return (query_gradient, jnp.concatenate([key_gradient, value_gradient], axis=-1))


def window_rows(values, windows):
    levels, lat_rows, columns, per_dev, inner = values.shape
    shaped = values.reshape(levels, windows, WIN_LAT, columns, per_dev, inner)
    return shaped.transpose(4, 1, 0, 2, 3, 5).reshape(
        per_dev * windows, levels * WIN_LAT * columns, inner
    )


def unwindow_rows(values, levels, windows, columns, per_dev):
    inner = values.shape[-1]
    shaped = values.reshape(per_dev, windows, levels, WIN_LAT, columns, inner).transpose(
        2, 1, 3, 4, 0, 5
    )
    return shaped.reshape(levels, windows * WIN_LAT, columns, per_dev, inner)


def window_keys(kv_ext, windows):
    levels, lat_rows, key_cols, per_dev, inner = kv_ext.shape
    half_lat = WIN_LAT // 2
    padded = jnp.pad(kv_ext, ((0, 0), (half_lat, half_lat), (0, 0), (0, 0), (0, 0)))
    lower = padded[:, :lat_rows].reshape(levels, windows, WIN_LAT, key_cols, per_dev, inner)
    upper = padded[:, WIN_LAT : lat_rows + WIN_LAT].reshape(
        levels, windows, WIN_LAT, key_cols, per_dev, inner
    )
    joined = jnp.concatenate([lower, upper], axis=2)
    return joined.transpose(4, 1, 0, 2, 3, 5).reshape(
        per_dev * windows, levels * 2 * WIN_LAT * key_cols, inner
    )


def unwindow_keys(grads, levels, windows, key_cols, per_dev):
    inner = grads.shape[-1]
    lat_rows = windows * WIN_LAT
    half_lat = WIN_LAT // 2
    shaped = grads.reshape(per_dev, windows, levels, 2 * WIN_LAT, key_cols, inner).transpose(
        2, 1, 3, 4, 0, 5
    )
    lower = shaped[:, :, :WIN_LAT].reshape(levels, lat_rows, key_cols, per_dev, inner)
    upper = shaped[:, :, WIN_LAT:].reshape(levels, lat_rows, key_cols, per_dev, inner)
    summed = jnp.pad(lower, ((0, 0), (0, WIN_LAT), (0, 0), (0, 0), (0, 0))) + jnp.pad(
        upper, ((0, 0), (WIN_LAT, 0), (0, 0), (0, 0), (0, 0))
    )
    return summed[:, half_lat : half_lat + lat_rows]


def key_valid(levels, windows, key_cols, per_dev, lat_rows):
    lat_index = (
        WIN_LAT * jnp.arange(windows)[:, None] - WIN_LAT // 2 + jnp.arange(2 * WIN_LAT)[None, :]
    )
    inside = (lat_index >= 0) & (lat_index < lat_rows)
    spread = jnp.broadcast_to(
        inside[None, :, None, :, None], (per_dev, windows, levels, 2 * WIN_LAT, key_cols)
    )
    return spread.reshape(per_dev * windows, -1)


def to_blocks(values):
    return values.reshape((values.shape[0] // 4, 4) + values.shape[1:])


def from_blocks(values):
    return values.reshape((-1,) + values.shape[2:])


def body(latents, out_grad, qkv_weight, out_weight):
    levels, lat_dev, columns, model_width = latents.shape
    groups = lax.axis_size("head")
    lat_rows = lat_dev * groups
    per_dev = qkv_weight.shape[0]
    head_count = out_weight.shape[0]
    head_width = out_weight.shape[1]
    score_scale_factor = head_width ** (-0.5)
    windows = lat_rows // WIN_LAT
    half_lon = WIN_LON // 2
    out_flat = out_weight.reshape(head_count * head_width, model_width)
    band_rows = lax.all_gather(latents, "head", axis=1, tiled=True)
    projected = jnp.einsum(
        "lawd,hdc->lawhc", band_rows, qkv_weight, preferred_element_type=jnp.float32
    ).astype(jnp.bfloat16)
    kv_ext = extended(projected[..., head_width:], (("lon", 2),), half_lon)
    key_cols = kv_ext.shape[2]
    query_rows = window_rows(projected[..., :head_width], windows)
    key_value_pairs = window_keys(kv_ext, windows)
    valid = key_valid(levels, windows, key_cols, per_dev, lat_rows)
    attended_values = lax.map(
        lambda pack: attend_block(pack, head_width, score_scale_factor),
        (to_blocks(query_rows), to_blocks(key_value_pairs), to_blocks(valid)),
    )
    attended_values = unwindow_rows(from_blocks(attended_values), levels, windows, columns, per_dev)
    attended_values = attended_values.reshape(levels, lat_rows, columns, per_dev * head_width)
    token_attended = lax.all_to_all(
        attended_values, "head", split_axis=1, concat_axis=3, tiled=True
    )
    mixed = jnp.dot(
        token_attended.reshape(-1, head_count * head_width),
        out_flat,
        preferred_element_type=jnp.float32,
    )
    mixed = mixed.astype(jnp.bfloat16).reshape(latents.shape)
    token_grad = jnp.dot(
        out_grad.reshape(-1, model_width), out_flat.T, preferred_element_type=jnp.float32
    ).astype(jnp.bfloat16)
    token_grad = token_grad.reshape(levels, lat_dev, columns, head_count * head_width)
    band_grad = lax.all_to_all(token_grad, "head", split_axis=3, concat_axis=1, tiled=True)
    band_grad = window_rows(
        band_grad.reshape(levels, lat_rows, columns, per_dev, head_width), windows
    )
    query_gradient, pair_grad = lax.map(
        lambda pack: attend_grad(pack, head_width, score_scale_factor),
        (to_blocks(query_rows), to_blocks(key_value_pairs), to_blocks(valid), to_blocks(band_grad)),
    )
    query_gradient = unwindow_rows(from_blocks(query_gradient), levels, windows, columns, per_dev)
    ext_grad = unwindow_keys(from_blocks(pair_grad), levels, windows, key_cols, per_dev)
    west_edge = ext_grad[:, :, half_lon + columns :].astype(jnp.bfloat16)
    east_edge = ext_grad[:, :, :half_lon].astype(jnp.bfloat16)
    from_west = shifted(west_edge, "lon", 1).astype(jnp.float32)
    from_east = shifted(east_edge, "lon", -1).astype(jnp.float32)
    own_grad = ext_grad[:, :, half_lon : half_lon + columns]
    own_grad = own_grad + jnp.pad(
        from_west, ((0, 0), (0, 0), (0, columns - half_lon), (0, 0), (0, 0))
    )
    own_grad = own_grad + jnp.pad(
        from_east, ((0, 0), (0, 0), (columns - half_lon, 0), (0, 0), (0, 0))
    )
    projected_grad = jnp.concatenate([query_gradient, own_grad], axis=-1).astype(jnp.bfloat16)
    grad_tokens = lax.all_to_all(
        projected_grad.reshape(levels, lat_rows, columns, per_dev * 3 * head_width),
        "head",
        split_axis=1,
        concat_axis=3,
        tiled=True,
    )
    grad_flat = grad_tokens.reshape(-1, head_count * 3 * head_width)
    piece = lax.all_gather(qkv_weight, "head", axis=0, tiled=True)
    part_cols = grad_flat
    part_cols = part_cols.reshape(grad_flat.shape[0], piece.shape[0], 3 * head_width)
    latent_sum = jnp.einsum("rnc,ndc->rd", part_cols, piece, preferred_element_type=jnp.float32)
    local_grad = jnp.einsum(
        "lawd,lawhc->hdc", band_rows, projected_grad, preferred_element_type=jnp.float32
    )
    latent_grad = latent_sum.astype(jnp.bfloat16).reshape(latents.shape)
    qkv_grad = lax.psum(local_grad.astype(jnp.bfloat16), "lon").astype(jnp.float32)
    return (mixed, latent_grad, qkv_grad)


def solution(mesh):
    placed = (
        P(None, "head", "lon", None),
        P(None, "head", "lon", None),
        P("head", None, None),
        P(),
    )
    return jax.shard_map(
        body,
        mesh=mesh,
        in_specs=placed,
        out_specs=(
            P(None, "head", "lon", None),
            P(None, "head", "lon", None),
            P("head", None, None),
        ),
        check_vma=False,
    )
```

profile of v0, /device:TPU:1, one launch (start us, length us, event | category | flops | bytes accessed | tf_op | source)
XLA Modules:
  0.0 604.0 jit_solution(525923004497261333)
XLA Ops:
  8.8 1.7 convolution_convert_fusion.2
  10.4 3.6 copy.69
  14.1 5.8 reshape.129
  19.9 12.0 %all-to-all-start.1 = ((bf16[16,2,2304]{2,1,0:T(2,128)(2,1)}), bf16[16,2,2304]{2,1,0:T(2,128)(2,1)S(1)}, u32[]{:S(2)}, u32[]{:S(2)}) async-start(bf16[16,2,2304]{2,1,0:T(2,128)(2,1)} %reshape.129), calls=%async_computation.1 | async-start | bytes 294912 | tf_op jit(solution)/shard_map/all_to_all | solution.py:183
  31.9 54.7 %all-gather.3.cloned.1.call-done = bf16[3,48,8,1024]{3,2,1,0:T(8,128)(2,1)} async-done(((bf16[3,3,8,1024]{3,2,1,0:T(8,128)(2,1)}), bf16[3,48,8,1024]{3,2,1,0:T(8,128)(2,1)}) %all-gather.3.cloned.1.call-update) | async-done | bytes 2359312 | tf_op jit(solution)/shard_map/all_gather | solution.py:155
  86.6 2.5 fusion.87
  89.1 1.0 fusion.119
  90.1 11.9 %collective-permute-start.1 = (bf16[3,48,4,1,128]{4,2,1,0,3:T(4,128)(2,1)}, bf16[3,48,4,1,128]{4,2,1,0,3:T(4,128)(2,1)}, u32[]{:S(2)}, u32[]{:S(2)}) collective-permute-start(bf16[3,48,4,1,128]{4,2,1,0,3:T(4,128)(2,1)} %get-tuple-element.142), channel_id=1, source_target_pairs={{16,0},{32,16},{48,32},{64,48},{80,64},{96,80},{112,96},{128,112},... | collective-permute-start | bytes 442376 | tf_op jit(solution)/shard_map/ppermute | solution.py:20
  102.0 3.8 collective-permute-start
  106.2 3.9 reshape.130
  110.1 3.9 copy.92
  115.2 1.0 copy.63
  116.2 1.3 fusion.96
  117.8 1.2 copy.90
  119.0 1.7 copy.64
  120.7 26.0 %while.23 = (s32[]{:T(128)}, bf16[2,4,144,64]{2,3,1,0:T(8,128)(2,1)}, f32[2,4,576,128]{3,2,1,0:T(8,128)}, pred[2,4,576]{2,1,0:T(4,128)(4,1)S(1)}, bf16[2,4,144,6...) while((s32[]{:T(128)}, ...), condition=%wide.region_8.9_spmd, body=%wide.region_4.8_spmd.sunk | while | flops 217128960 | bytes 40974684 | solution.py:187
  120.7 1.0 dynamic-slice_bitcast_fusion.11
  121.7 2.9 fusion.162
  124.6 2.2 multiply_reduce_fusion.2
  129.8 1.4 copy.111
  131.2 2.5 constant_dynamic-update-slice_fusion.2
  133.7 1.0 dynamic-slice_bitcast_fusion.11
  134.7 2.9 fusion.162
  137.6 2.2 multiply_reduce_fusion.2
  142.8 1.4 copy.111
  144.2 2.5 constant_dynamic-update-slice_fusion.2
  146.7 1.8 fusion.116
  151.8 1.9 collective-permute-start.3
  153.7 4.7 collective-permute-start.2
  158.4 1.8 copy.76
  160.3 1.1 copy.77
  161.6 1.6 fusion.102
  163.9 2.7 fusion.88
  167.4 11.0 %while.22 = (s32[]{:T(128)}, bf16[2,4,144,64]{2,3,1,0:T(8,128)(2,1)}, pred[2,4,576]{2,1,0:T(4,128)(4,1)S(1)}, bf16[2,4,144,64]{2,3,1,0:T(8,128)(2,1)}, bf16[2,4,576,128]{2,3,1,0:T(8,128)(2,1)S(1)}, /*index=5*/s32[]{:T(128)}) while((s32[]{:T(128)}, bf16[2,4,144,64]{2,3,1,0:T(8,128)(2,1)}, pred[2,4,576]{2,1,0:T(4,128)(4,1)S(1)}, ...), condition=%wide.region_3.4_spmd, body=%wide.region_0.3_spmd.sunk | while | flops 130426560 | bytes 2570841 | solution.py:164
  168.3 1.8 fusion.152
  170.2 2.7 fusion.153
  173.8 1.8 fusion.152
  175.6 2.7 fusion.153
  178.4 1.2 copy.65
  180.5 4.3 all-to-all-start
  185.1 1.0 copy.84
  186.1 6.7 %all-to-all-done = bf16[16,2,2304]{2,1,0:T(2,128)(2,1)S(1)} async-done(((bf16[16,2,2304]{2,1,0:T(2,128)(2,1)}), bf16[16,2,2304]{2,1,0:T(2,128)(2,1)S(1)}, u32[]{:S(2)}, u32[]{:S(2)}) %all-to-all-start) | async-done | bytes 147488 | tf_op jit(solution)/shard_map/all_to_all | solution.py:170
  192.8 3.6 all-to-all-start.2
  196.9 1.1 convolution_convert_fusion.3
  198.0 249.5 %all-reduce.7.cloned.1.call-done = bf16[1,1024,192]{1,2,0:T(8,128)(2,1)} async-done(((bf16[1,1024,192]{1,2,0:T(8,128)(2,1)}), bf16[1,1024,192]{1,2,0:T(8,128)(2,1)}) %all-reduce.7.cloned.1.call-update) | async-done | bytes 393232 | tf_op jit(solution)/shard_map/psum | solution.py:221
  447.5 2.0 convert_element_type.66
  449.5 143.2 %all-gather.5.cloned.1.call-done = bf16[16,1024,192]{1,2,0:T(8,128)(2,1)} async-done(((bf16[1,1024,192]{1,2,0:T(8,128)(2,1)}), bf16[16,1024,192]{1,2,0:T(8,128)(2,1)}) %all-gather.5.cloned.1.call-update) | async-done | bytes 6291472 | tf_op jit(solution)/shard_map/all_gather | solution.py:213
  592.8 4.7 fusion.91
  (109 shorter events, 17.7 us)
Async XLA Ops:
  7.2 1.6 copy-start
  7.2 79.4 %all-gather.3.cloned.1.call-start = ((), (), s32[]{:S(2)}) async-start(), calls=%async_computation.3 | async-start | bytes 2506752 | tf_op jit(solution)/shard_map/all_gather | solution.py:155
  14.1 72.5 %copy-start.13 = (bf16[1,1024,192]{1,2,0:T(8,128)(2,1)S(1)}, bf16[1,1024,192]{1,2,0:T(8,128)(2,1)}, u32[]{:S(2)}) copy-start(bf16[1,1024,192]{1,2,0:T(8,128)(2,1)} %param.10) | copy-start | bytes 1179652
  19.9 86.3 %all-to-all-start.1 = ((bf16[16,2,2304]{2,1,0:T(2,128)(2,1)}), bf16[16,2,2304]{2,1,0:T(2,128)(2,1)S(1)}, u32[]{:S(2)}, u32[]{:S(2)}) async-start(bf16[16,2,2304]{2,1,0:T(2,128)(2,1)} %reshape.129), calls=%async_computation.1 | async-start | bytes 294912 | tf_op jit(solution)/shard_map/all_to_all | solution.py:183
  31.8 415.7 %all-reduce.7.cloned.1.call-start = ((), (), s32[]{:S(2)}) async-start(), calls=%async_computation.5 | async-start | bytes 786432 | tf_op jit(solution)/shard_map/psum | solution.py:221
  90.1 26.0 %collective-permute-start.1 = (bf16[3,48,4,1,128]{4,2,1,0,3:T(4,128)(2,1)}, bf16[3,48,4,1,128]{4,2,1,0,3:T(4,128)(2,1)}, u32[]{:S(2)}, u32[]{:S(2)}) collective-permute-start(bf16[3,48,4,1,128]{4,2,1,0,3:T(4,128)(2,1)} %get-tuple-element.142), channel_id=1, source_target_pairs={{16,0},{32,16},{48,32},{64,48},{80,64},{96,80},{112,96},{128,112},... | collective-permute-start | bytes 442376 | tf_op jit(solution)/shard_map/ppermute | solution.py:20
  102.0 14.1 %collective-permute-start = (bf16[3,48,4,1,128]{4,2,1,0,3:T(4,128)(2,1)}, bf16[3,48,4,1,128]{4,2,1,0,3:T(4,128)(2,1)}, u32[]{:S(2)}, u32[]{:S(2)}) collective-permute-start(bf16[3,48,4,1,128]{4,2,1,0,3:T(4,128)(2,1)} %get-tuple-element.141), channel_id=1, source_target_pairs={{0,16},{16,32},{32,48},{48,64},{64,80},{80,96},{96,112},{112,128},... | collective-permute-start | bytes 442376 | tf_op jit(solution)/shard_map/ppermute | solution.py:17
  120.7 3.9 copy-start.1
  124.6 2.2 copy-start.3
  126.8 1.1 copy-start.4
  126.8 1.1 copy-start.15
  126.8 1.6 copy-start.14
  128.4 0.7 copy-start.16
  128.4 1.0 copy-start.8
  131.2 2.5 copy-start.2
  133.7 3.9 copy-start.1
  137.6 2.2 copy-start.3
  139.8 1.1 copy-start.4
  139.8 1.1 copy-start.15
  139.8 1.6 copy-start.14
  141.3 0.7 copy-start.16
  141.4 1.0 copy-start.8
  144.2 2.5 copy-start.2
  148.9 1.0 copy-start.5
  150.0 1.0 copy-start.7
  151.8 9.6 %collective-permute-start.3 = (bf16[3,48,4,1,128]{4,1,2,0,3:T(8,128)(2,1)}, bf16[3,48,4,1,128]{4,1,2,0,3:T(8,128)(2,1)}, u32[]{:S(2)}, u32[]{:S(2)}) collective-permute-start(bf16[3,48,4,1,128]{4,1,2,0,3:T(8,128)(2,1)} %get-tuple-element.138), channel_id=1, source_target_pairs={{16,0},{32,16},{48,32},{64,48},{80,64},{96,80},{112,96},{128,112},... | collective-permute-start | bytes 442376 | tf_op jit(solution)/shard_map/ppermute | solution.py:28
  153.7 7.7 %collective-permute-start.2 = (bf16[3,48,4,1,128]{4,1,2,0,3:T(8,128)(2,1)}, bf16[3,48,4,1,128]{4,1,2,0,3:T(8,128)(2,1)}, u32[]{:S(2)}, u32[]{:S(2)}) collective-permute-start(bf16[3,48,4,1,128]{4,1,2,0,3:T(8,128)(2,1)} %get-tuple-element.137), channel_id=1, source_target_pairs={{496,0},{0,16},{16,32},{32,48},{48,64},{64,80},{80,96},{96,112},{1... | collective-permute-start | bytes 442376 | tf_op jit(solution)/shard_map/ppermute | solution.py:28
  160.3 1.4 copy-start.6
  161.4 1.8 copy-start.11
  161.4 2.5 copy-start.17
  163.2 0.7 copy-start.9
  166.6 426.1 %all-gather.5.cloned.1.call-start = ((), (), s32[]{:S(2)}) async-start(), calls=%async_computation.4 | async-start | bytes 6684672 | tf_op jit(solution)/shard_map/all_gather | solution.py:213
  178.3 6.4 %copy-start.10 = (bf16[3,48,8,128]{3,1,2,0:T(8,128)(2,1)S(1)}, bf16[3,48,8,128]{3,1,2,0:T(8,128)(2,1)}, u32[]{:S(2)}) copy-start(bf16[3,48,8,128]{3,1,2,0:T(8,128)(2,1)} %copy-done.9) | copy-start | bytes 884740
  178.3 6.5 %copy-start.12 = (bf16[3,48,8,64]{3,1,2,0:T(8,128)(2,1)S(1)}, bf16[3,48,8,64]{3,1,2,0:T(8,128)(2,1)}, u32[]{:S(2)}) copy-start(bf16[3,48,8,64]{3,1,2,0:T(8,128)(2,1)} %copy-done.11) | copy-start | bytes 442372
  180.5 12.3 %all-to-all-start = ((bf16[16,2,2304]{2,1,0:T(2,128)(2,1)}), bf16[16,2,2304]{2,1,0:T(2,128)(2,1)S(1)}, u32[]{:S(2)}, u32[]{:S(2)}) async-start(bf16[16,2,2304]{2,1,0:T(2,128)(2,1)} %reshape.127), calls=%async_computation | async-start | bytes 294912 | tf_op jit(solution)/shard_map/all_to_all | solution.py:170
  192.8 256.7 %all-to-all-start.2 = ((bf16[3,48,8,192]{3,2,0,1:T(8,128)(2,1)}), bf16[3,48,8,192]{3,2,0,1:T(8,128)(2,1)S(1)}, u32[]{:S(2)}, u32[]{:S(2)}) async-start(bf16[3,48,8,192]{3,2,0,1:T(8,128)(2,1)} %copy.84), calls=%async_computation.2 | async-start | bytes 1179648 | tf_op jit(solution)/shard_map/all_to_all | solution.py:205
Sparse Core Ops, SparseCore 0:
  10.1 76.4 all-gather.2
  166.8 280.7 all-reduce.6
  449.6 143.1 all-gather.4
where the time goes:
time: 605 us; the launch traced here: 604 us
  waiting for transfers between devices  456 us (75%)
  local copies, waits for them, and re-layouts  51.7 us (9%)
  starting transfers between devices  42.3 us (7%)
  matrix products  33.9 us (6%)
  between operations  14.1 us (2%)
  other arithmetic  6.22 us (1%)
    psum x1, waiting for transfers between devices, body(): lax.psum(local_grad.astype(jnp.bfloat16), 'lon').astype(jnp.float32)  250 us
    all_gather x1, waiting for transfers between devices, body(): piece = lax.all_gather(qkv_weight, 'head', axis=0, tiled=True)  143 us
    all_gather x1, waiting for transfers between devices, body(): band_rows = lax.all_gather(latents, 'head', axis=1, tiled=True)  54.7 us
    unnamed x24, local copies, waits for them, and re-layouts  13.9 us
  transfers between devices with their start and end apart: 10, of which 4 were waited for; matrix products, arithmetic and copies ran while one was open for 8% of the time, Pallas kernels for 0%

commit v1 on v0

--- a/solution.py
+++ b/solution.py
@@ -218,7 +218,9 @@
         "lawd,lawhc->hdc", band_rows, projected_grad, preferred_element_type=jnp.float32
     )
     latent_grad = latent_sum.astype(jnp.bfloat16).reshape(latents.shape)
-    qkv_grad = lax.psum(local_grad.astype(jnp.bfloat16), "lon").astype(jnp.float32)
+    qkv_grad = jnp.sum(lax.all_gather(local_grad.astype(jnp.bfloat16), "lon"), axis=0).astype(
+        jnp.float32
+    )
     return (mixed, latent_grad, qkv_grad)
 
 

time: 605 us -> 374 us (0.62)
  waiting for transfers between devices: 456 us -> 218 us
  other arithmetic: 6.22 us -> 12.9 us
    psum x1 -> x0, waiting for transfers between devices: 250 us -> none  [body(): lax.psum(local_grad.astype(jnp.bfloat16), 'lon').astype(jnp.float32)]
    all_gather x1, waiting for transfers between devices: 143 us -> 38.4 us  [body(): piece = lax.all_gather(qkv_weight, 'head', axis=0, tiled=True)]
    all_gather x0 -> x1, waiting for transfers between devices: none -> 99 us  [body(): lax.all_gather(local_grad.astype(jnp.bfloat16), 'lon')]
    all_to_all x1, waiting for transfers between devices: 0.01 us -> 12.9 us  [body(): lax.all_to_all(projected_grad.reshape(levels, lat_rows, columns, per_dev...]
    reduce_sum x0 -> x1, other arithmetic: none -> 7.87 us  [body(): jnp.sum(lax.all_gather(local_grad.astype(jnp.bfloat16), 'lon'), axis=0)]
  transfers between devices with their start and end apart: 10 -> 10, of which waited for: 4 -> 6; matrix products, arithmetic and copies ran while one was open for 8% -> 22% of each run, Pallas kernels for 0% -> 0%
where the time goes in v1:
time: 374 us; the launch traced here: 372 us
  waiting for transfers between devices  218 us (58%)
  local copies, waits for them, and re-layouts  50.8 us (14%)
  starting transfers between devices  42.3 us (11%)
  matrix products  34 us (9%)
  between operations  14.1 us (4%)
  other arithmetic  12.9 us (3%)
    all_gather x1, waiting for transfers between devices, body(): lax.all_gather(local_grad.astype(jnp.bfloat16), 'lon')  99 us
    all_gather x1, waiting for transfers between devices, body(): band_rows = lax.all_gather(latents, 'head', axis=1, tiled=True)  54.7 us
    all_gather x1, waiting for transfers between devices, body(): piece = lax.all_gather(qkv_weight, 'head', axis=0, tiled=True)  38.4 us
    unnamed x24, local copies, waits for them, and re-layouts  13 us
    all_to_all x1, waiting for transfers between devices, body(): lax.all_to_all(projected_grad.reshape(levels, lat_rows, columns, per_dev...  12.9 us
    all_to_all x1, starting transfers between devices, body(): lax.all_to_all(token_grad, 'head', split_axis=3, concat_axis=1, tiled=True)  12 us
    ppermute x1, starting transfers between devices, extended(): lax.ppermute(lax.slice_in_dim(block, 0, width, axis=dim), axis, backward)  11.9 us
    sub x4, matrix products, softmax_rows(): powers = jnp.exp(score_matrix - row_max)  9.46 us
  transfers between devices with their start and end apart: 10, of which 6 were waited for; matrix products, arithmetic and copies ran while one was open for 22% of the time, Pallas kernels for 0%

profile of v1, /device:TPU:1, one launch (start us, length us, event | category | flops | bytes accessed | tf_op | source)
XLA Modules:
  0.0 372.3 jit_solution(4737780354678923580)
XLA Ops:
  8.8 1.7 convolution_convert_fusion.2
  10.4 3.6 copy.69
  14.1 5.8 %reshape.144 = bf16[16,2,2304]{2,1,0:T(2,128)(2,1)} reshape(bf16[1024,3,3,8]{3,2,1,0:T(4,128)(2,1)} %bitcast.171) | data formatting | bytes 294912
  19.9 12.0 %all-to-all-start.1 = ((bf16[16,2,2304]{2,1,0:T(2,128)(2,1)}), bf16[16,2,2304]{2,1,0:T(2,128)(2,1)S(1)}, u32[]{:S(2)}, u32[]{:S(2)}) async-start(bf16[16,2,2304]{2,1,0:T(2,128)(2,1)} %reshape.144), calls=%async_computation.1 | async-start | bytes 294912 | tf_op jit(solution)/shard_map/all_to_all | solution.py:183
  31.9 54.7 %all-gather.5.cloned.1.call-done = bf16[3,48,8,1024]{3,2,1,0:T(8,128)(2,1)} async-done(((bf16[3,3,8,1024]{3,2,1,0:T(8,128)(2,1)}), bf16[3,48,8,1024]{3,2,1,0:T(8,128)(2,1)}) %all-gather.5.cloned.1.call-update) | async-done | bytes 2359312 | tf_op jit(solution)/shard_map/all_gather | solution.py:155
  86.6 2.5 fusion.87
  89.1 1.0 fusion.119
  90.1 11.9 %collective-permute-start.1 = (bf16[3,48,4,1,128]{4,2,1,0,3:T(4,128)(2,1)}, bf16[3,48,4,1,128]{4,2,1,0,3:T(4,128)(2,1)}, u32[]{:S(2)}, u32[]{:S(2)}) collective-permute-start(bf16[3,48,4,1,128]{4,2,1,0,3:T(4,128)(2,1)} %get-tuple-element.142), channel_id=1, source_target_pairs={{16,0},{32,16},{48,32},{64,48},{80,64},{96,80},{112,96},{128,112},... | collective-permute-start | bytes 442376 | tf_op jit(solution)/shard_map/ppermute | solution.py:20
  102.0 3.8 %collective-permute-start = (bf16[3,48,4,1,128]{4,2,1,0,3:T(4,128)(2,1)}, bf16[3,48,4,1,128]{4,2,1,0,3:T(4,128)(2,1)}, u32[]{:S(2)}, u32[]{:S(2)}) collective-permute-start(bf16[3,48,4,1,128]{4,2,1,0,3:T(4,128)(2,1)} %get-tuple-element.141), channel_id=1, source_target_pairs={{0,16},{16,32},{32,48},{48,64},{64,80},{80,96},{96,112},{112,128},... | collective-permute-start | bytes 442376 | tf_op jit(solution)/shard_map/ppermute | solution.py:17
  106.2 3.9 %reshape.145 = bf16[1024,3,3,8]{3,2,1,0:T(4,128)(2,1)} reshape(bf16[16,2,2304]{2,1,0:T(2,128)(2,1)S(1)} %all-to-all-done.1) | data formatting | bytes 294912
  110.1 4.0 %copy.92 = bf16[3,3,8,16,64]{4,2,1,3,0:T(8,128)(2,1)S(1)} copy(bf16[3,3,8,16,64]{2,1,0,4,3:T(4,128)(2,1)} %bitcast.172) | data formatting | bytes 294912 | tf_op jit(solution)/shard_map/all_to_all | solution.py:183
  116.1 1.3 fusion.96
  117.7 1.2 copy.90
  119.0 1.7 copy.64
  120.6 26.1 %while.23 = (s32[]{:T(128)}, bf16[2,4,144,64]{2,3,1,0:T(8,128)(2,1)}, f32[2,4,576,128]{3,2,1,0:T(8,128)}, pred[2,4,576]{2,1,0:T(4,128)(4,1)S(1)}, bf16[2,4,144,6...) while((s32[]{:T(128)}, ...), condition=%wide.region_8.9_spmd, body=%wide.region_4.8_spmd.sunk | while | flops 217128960 | bytes 40974684 | solution.py:187
  120.7 1.0 dynamic-slice_bitcast_fusion.11
  121.7 2.9 fusion.162
  124.6 2.2 multiply_reduce_fusion.2
  129.8 1.4 copy.111
  131.2 2.5 constant_dynamic-update-slice_fusion.2
  133.7 1.0 dynamic-slice_bitcast_fusion.11
  134.8 2.9 fusion.162
  137.6 2.2 multiply_reduce_fusion.2
  142.8 1.4 copy.111
  144.3 2.5 constant_dynamic-update-slice_fusion.2
  146.7 1.8 fusion.116
  151.9 1.9 collective-permute-start.3
  153.8 4.7 %collective-permute-start.2 = (bf16[3,48,4,1,128]{4,1,2,0,3:T(8,128)(2,1)}, bf16[3,48,4,1,128]{4,1,2,0,3:T(8,128)(2,1)}, u32[]{:S(2)}, u32[]{:S(2)}) collective-permute-start(bf16[3,48,4,1,128]{4,1,2,0,3:T(8,128)(2,1)} %get-tuple-element.137), channel_id=1, source_target_pairs={{496,0},{0,16},{16,32},{32,48},{48,64},{64,80},{80,96},{96,112},{1... | collective-permute-start | bytes 442376 | tf_op jit(solution)/shard_map/ppermute | solution.py:28
  158.5 1.8 copy.76
  160.3 1.1 copy.77
  161.5 4.1 %collective-permute-done.2 = bf16[3,48,4,1,128]{4,1,2,0,3:T(8,128)(2,1)} collective-permute-done((bf16[3,48,4,1,128]{4,1,2,0,3:T(8,128)(2,1)}, bf16[3,48,4,1,128]{4,1,2,0,3:T(8,128)(2,1)}, u32[]{:S(2)}, u32[]{:S(2)}) %collective-permute-start.2) | collective-permute-done | bytes 147488 | tf_op jit(solution)/shard_map/ppermute | solution.py:28
  165.6 1.4 fusion.102
  167.7 2.7 fusion.88
  170.4 11.0 %while.22 = (s32[]{:T(128)}, bf16[2,4,144,64]{2,3,1,0:T(8,128)(2,1)}, pred[2,4,576]{2,1,0:T(4,128)(4,1)S(1)}, bf16[2,4,144,64]{2,3,1,0:T(8,128)(2,1)}, bf16[2,4,576,128]{2,3,1,0:T(8,128)(2,1)S(1)}, /*index=5*/s32[]{:T(128)}) while((s32[]{:T(128)}, bf16[2,4,144,64]{2,3,1,0:T(8,128)(2,1)}, pred[2,4,576]{2,1,0:T(4,128)(4,1)S(1)}, ...), condition=%wide.region_3.4_spmd, body=%wide.region_0.3_spmd.sunk | while | flops 130426560 | bytes 2570841 | solution.py:164
  171.3 1.8 fusion.152
  173.2 2.7 fusion.153
  176.8 1.8 fusion.152
  178.6 2.7 fusion.153
  181.4 1.2 copy.65
  183.5 4.2 %all-to-all-start = ((bf16[16,2,2304]{2,1,0:T(2,128)(2,1)}), bf16[16,2,2304]{2,1,0:T(2,128)(2,1)S(1)}, u32[]{:S(2)}, u32[]{:S(2)}) async-start(bf16[16,2,2304]{2,1,0:T(2,128)(2,1)} %reshape.142), calls=%async_computation | async-start | bytes 294912 | tf_op jit(solution)/shard_map/all_to_all | solution.py:170
  189.1 7.6 %all-to-all-done = bf16[16,2,2304]{2,1,0:T(2,128)(2,1)S(1)} async-done(((bf16[16,2,2304]{2,1,0:T(2,128)(2,1)}), bf16[16,2,2304]{2,1,0:T(2,128)(2,1)S(1)}, u32[]{:S(2)}, u32[]{:S(2)}) %all-to-all-start) | async-done | bytes 147488 | tf_op jit(solution)/shard_map/all_to_all | solution.py:170
  196.6 3.6 all-to-all-start.2
  200.7 1.2 convolution_convert_fusion.3
  201.8 12.9 %all-to-all-done.2 = bf16[3,48,8,192]{3,2,0,1:T(8,128)(2,1)S(1)} async-done(((bf16[3,48,8,192]{3,2,0,1:T(8,128)(2,1)}), bf16[3,48,8,192]{3,2,0,1:T(8,128)(2,1)S(1)}, u32[]{:S(2)}, u32[]{:S(2)}) %all-to-all-start.2) | async-done | bytes 442400 | tf_op jit(solution)/shard_map/all_to_all | solution.py:205
  214.8 38.4 %all-gather.7.cloned.1.call-done = bf16[16,1024,192]{1,2,0:T(8,128)(2,1)} async-done(((bf16[1,1024,192]{1,2,0:T(8,128)(2,1)}), bf16[16,1024,192]{1,2,0:T(8,128)(2,1)}) %all-gather.7.cloned.1.call-update) | async-done | bytes 6291472 | tf_op jit(solution)/shard_map/all_gather | solution.py:213
  253.2 4.7 %fusion.91 = bf16[72,1024]{1,0:T(8,128)(2,1)} fusion(bf16[72,16,192]{2,0,1:T(8,128)(2,1)S(1)} %bitcast.173, bf16[16,1024,192]{1,2,0:T(8,128)(2,1)} %all-gather.7.cloned.1.call-done), kind=kOutput, calls=%fused_computation.77 | convolution fusion | flops 453058560 | bytes 6881280 | tf_op jit(solution)/shard_map/rnc,ndc->rd/dot_general | solution.py:216
  257.9 99.0 %all-gather.9.cloned.1.call-done = bf16[32,1024,192]{1,2,0:T(8,128)(2,1)} async-done(((bf16[1,1024,192]{1,2,0:T(8,128)(2,1)}), bf16[32,1024,192]{1,2,0:T(8,128)(2,1)}) %all-gather.9.cloned.1.call-update) | async-done | bytes 12582928 | tf_op jit(solution)/shard_map/all_gather | solution.py:221
  356.9 7.9 %reduce.2 = bf16[1024,192]{0,1:T(8,128)(2,1)S(1)} reduce(bf16[32,1024,192]{1,2,0:T(8,128)(2,1)} %all-gather.9.cloned.1.call-done, bf16[]{:T(256)} %constant.59.clone.1), dimensions={0}, to_apply=%region_9.10 | reduce | flops 6094848 | bytes 12976130 | tf_op jit(solution)/shard_map/reduce_sum | solution.py:221
  (110 shorter events, 19.6 us)
Async XLA Ops:
  7.2 1.6 copy-start
  7.2 79.4 %all-gather.5.cloned.1.call-start = ((), (), s32[]{:S(2)}) async-start(), calls=%async_computation.3 | async-start | bytes 2506752 | tf_op jit(solution)/shard_map/all_gather | solution.py:155
  7.9 245.3 %all-gather.7.cloned.1.call-start = ((), (), s32[]{:S(2)}) async-start(), calls=%async_computation.4 | async-start | bytes 6684672 | tf_op jit(solution)/shard_map/all_gather | solution.py:213
  14.1 72.5 %copy-start.13 = (bf16[1,1024,192]{1,2,0:T(8,128)(2,1)S(1)}, bf16[1,1024,192]{1,2,0:T(8,128)(2,1)}, u32[]{:S(2)}) copy-start(bf16[1,1024,192]{1,2,0:T(8,128)(2,1)} %param.10) | copy-start | bytes 1179652
  19.9 86.3 %all-to-all-start.1 = ((bf16[16,2,2304]{2,1,0:T(2,128)(2,1)}), bf16[16,2,2304]{2,1,0:T(2,128)(2,1)S(1)}, u32[]{:S(2)}, u32[]{:S(2)}) async-start(bf16[16,2,2304]{2,1,0:T(2,128)(2,1)} %reshape.144), calls=%async_computation.1 | async-start | bytes 294912 | tf_op jit(solution)/shard_map/all_to_all | solution.py:183
  31.8 325.1 %all-gather.9.cloned.1.call-start = ((), (), s32[]{:S(2)}) async-start(), calls=%async_computation.5 | async-start | bytes 12976128 | tf_op jit(solution)/shard_map/all_gather | solution.py:221
  90.1 26.0 %collective-permute-start.1 = (bf16[3,48,4,1,128]{4,2,1,0,3:T(4,128)(2,1)}, bf16[3,48,4,1,128]{4,2,1,0,3:T(4,128)(2,1)}, u32[]{:S(2)}, u32[]{:S(2)}) collective-permute-start(bf16[3,48,4,1,128]{4,2,1,0,3:T(4,128)(2,1)} %get-tuple-element.142), channel_id=1, source_target_pairs={{16,0},{32,16},{48,32},{64,48},{80,64},{96,80},{112,96},{128,112},... | collective-permute-start | bytes 442376 | tf_op jit(solution)/shard_map/ppermute | solution.py:20
  102.0 14.1 %collective-permute-start = (bf16[3,48,4,1,128]{4,2,1,0,3:T(4,128)(2,1)}, bf16[3,48,4,1,128]{4,2,1,0,3:T(4,128)(2,1)}, u32[]{:S(2)}, u32[]{:S(2)}) collective-permute-start(bf16[3,48,4,1,128]{4,2,1,0,3:T(4,128)(2,1)} %get-tuple-element.141), channel_id=1, source_target_pairs={{0,16},{16,32},{32,48},{48,64},{64,80},{80,96},{96,112},{112,128},... | collective-permute-start | bytes 442376 | tf_op jit(solution)/shard_map/ppermute | solution.py:17
  120.7 4.0 %copy-start.1 = (bf16[2,4,576,128]{2,3,1,0:T(8,128)(2,1)}, bf16[2,4,576,128]{2,3,1,0:T(8,128)(2,1)S(1)}, u32[]{:S(2)}) copy-start(bf16[2,4,576,128]{2,3,1,0:T(8,128)(2,1)S(1)} %get-tuple-element.264) | copy-start | bytes 3538948 | tf_op jit(solution)/shard_map/while
  124.6 2.2 copy-start.3
  126.8 1.1 copy-start.4
  126.8 1.1 copy-start.15
  126.8 1.6 copy-start.14
  128.4 0.7 copy-start.16
  128.4 1.0 copy-start.8
  131.2 2.5 copy-start.2
  133.7 3.9 %copy-start.1 = (bf16[2,4,576,128]{2,3,1,0:T(8,128)(2,1)}, bf16[2,4,576,128]{2,3,1,0:T(8,128)(2,1)S(1)}, u32[]{:S(2)}) copy-start(bf16[2,4,576,128]{2,3,1,0:T(8,128)(2,1)S(1)} %get-tuple-element.264) | copy-start | bytes 3538948 | tf_op jit(solution)/shard_map/while
  137.6 2.2 copy-start.3
  139.8 1.1 copy-start.4
  139.8 1.1 copy-start.15
  139.8 1.6 copy-start.14
  141.4 0.7 copy-start.16
  141.4 1.0 copy-start.8
  144.3 2.5 copy-start.2
  149.0 1.0 copy-start.5
  150.0 1.0 copy-start.7
  151.9 9.6 %collective-permute-start.3 = (bf16[3,48,4,1,128]{4,1,2,0,3:T(8,128)(2,1)}, bf16[3,48,4,1,128]{4,1,2,0,3:T(8,128)(2,1)}, u32[]{:S(2)}, u32[]{:S(2)}) collective-permute-start(bf16[3,48,4,1,128]{4,1,2,0,3:T(8,128)(2,1)} %get-tuple-element.138), channel_id=1, source_target_pairs={{16,0},{32,16},{48,32},{64,48},{80,64},{96,80},{112,96},{128,112},... | collective-permute-start | bytes 442376 | tf_op jit(solution)/shard_map/ppermute | solution.py:28
  153.8 11.8 %collective-permute-start.2 = (bf16[3,48,4,1,128]{4,1,2,0,3:T(8,128)(2,1)}, bf16[3,48,4,1,128]{4,1,2,0,3:T(8,128)(2,1)}, u32[]{:S(2)}, u32[]{:S(2)}) collective-permute-start(bf16[3,48,4,1,128]{4,1,2,0,3:T(8,128)(2,1)} %get-tuple-element.137), channel_id=1, source_target_pairs={{496,0},{0,16},{16,32},{32,48},{48,64},{64,80},{80,96},{96,112},{1... | collective-permute-start | bytes 442376 | tf_op jit(solution)/shard_map/ppermute | solution.py:28
  160.3 5.2 %copy-start.6 = (f32[3,48,16,1,128]{4,1,2,0,3:T(8,128)S(1)}, f32[3,48,16,1,128]{4,1,2,0,3:T(8,128)}, u32[]{:S(2)}) copy-start(f32[3,48,16,1,128]{4,1,2,0,3:T(8,128)} %copy-done.5) | copy-start | bytes 3538948
  161.5 5.5 %copy-start.11 = (bf16[3,48,8,64]{3,1,2,0:T(8,128)(2,1)}, bf16[3,48,8,64]{3,1,2,0:T(8,128)(2,1)S(1)}, u32[]{:S(2)}) copy-start(bf16[3,48,8,64]{3,1,2,0:T(8,128)(2,1)S(1)} %copy.83) | copy-start | bytes 442372
  161.5 6.2 %copy-start.17 = (bf16[3,48,8,1024]{3,2,1,0:T(8,128)(2,1)S(1)}, bf16[3,48,8,1024]{3,2,1,0:T(8,128)(2,1)}, u32[]{:S(2)}) copy-start(bf16[3,48,8,1024]{3,2,1,0:T(8,128)(2,1)} %all-gather.5.cloned.1.call-done) | copy-start | bytes 7077892
  167.0 0.7 copy-start.9
  181.4 6.4 %copy-start.10 = (bf16[3,48,8,128]{3,1,2,0:T(8,128)(2,1)S(1)}, bf16[3,48,8,128]{3,1,2,0:T(8,128)(2,1)}, u32[]{:S(2)}) copy-start(bf16[3,48,8,128]{3,1,2,0:T(8,128)(2,1)} %copy-done.9) | copy-start | bytes 884740
  181.4 6.4 %copy-start.12 = (bf16[3,48,8,64]{3,1,2,0:T(8,128)(2,1)S(1)}, bf16[3,48,8,64]{3,1,2,0:T(8,128)(2,1)}, u32[]{:S(2)}) copy-start(bf16[3,48,8,64]{3,1,2,0:T(8,128)(2,1)} %copy-done.11) | copy-start | bytes 442372
  183.5 13.1 %all-to-all-start = ((bf16[16,2,2304]{2,1,0:T(2,128)(2,1)}), bf16[16,2,2304]{2,1,0:T(2,128)(2,1)S(1)}, u32[]{:S(2)}, u32[]{:S(2)}) async-start(bf16[16,2,2304]{2,1,0:T(2,128)(2,1)} %reshape.142), calls=%async_computation | async-start | bytes 294912 | tf_op jit(solution)/shard_map/all_to_all | solution.py:170
  196.6 18.2 %all-to-all-start.2 = ((bf16[3,48,8,192]{3,2,0,1:T(8,128)(2,1)}), bf16[3,48,8,192]{3,2,0,1:T(8,128)(2,1)S(1)}, u32[]{:S(2)}, u32[]{:S(2)}) async-start(bf16[3,48,8,192]{3,2,0,1:T(8,128)(2,1)} %copy.84), calls=%async_computation.2 | async-start | bytes 1179648 | tf_op jit(solution)/shard_map/all_to_all | solution.py:205
Sparse Core Ops, SparseCore 0:
  10.1 76.4 all-gather.4
  88.7 164.4 all-gather.6
  256.3 100.5 all-gather.8
